TPU v7x, 32 devices: a whole 2x2x4 slice. The times are simulated.
32 devices in a mesh: groups: 2 (over x), seq: 16 (over z, y, core).
Axes of the slice: x: 2, y: 2, z: 4, core: 2. Of those that a mesh axis runs over, the one named last changes fastest.
Arguments:
- tokens: bfloat16 [1024, 512, 512], P(('groups', 'seq')), parts along dimension 0, may hold values from -6 to 6
- cotangent: bfloat16 [1024, 512, 512], P('groups', 'seq'), parts along dimension 0, may hold values from -6 to 6
- w_first: bfloat16 [512, 512], P('seq'), may hold values from -0.25 to 0.25
- w_second: bfloat16 [512, 512], P('seq'), may hold values from -0.25 to 0.25
- mask_first: int32 [4, 4], replicated, may hold values from 0 to 1, as said below
- mask_second: int32 [4, 4], replicated, may hold values from 0 to 1, as said below
- gate_values: bfloat16 [1024, 512], P(('groups', 'seq')), parts along dimension 0, may hold values from -4 to 4
Outputs:
- grad_tokens: bfloat16 [1024, 512, 512], P(('groups', 'seq')), parts along dimension 0
- grad_first: float32 [1024, 512], P(('groups', 'seq')), parts along dimension 0
- grad_second: float32 [1024, 512], P(('groups', 'seq')), parts along dimension 0
There are 2 independent parts, one for each index of `groups`. A program takes and returns all parts, laid end to end along the dimension named above; an argument that names none is the same for every part. Nothing has to cross between parts.
Inputs may be any that keep to these rules, and one draw needn't show every extreme that they name: `mask_first`: the diagonal blocks of each factor are always kept. `mask_second`: the diagonal blocks of each factor are always kept.
All inputs are finite; a program needn't handle non-finite values.
Results may differ from a plain program's by a relative error of at most 0.0054.
Values may be sent and summed in bfloat16 or wider, within the bound.
A program may use at most 320 MiB of HBM per device.

v0:
```python
import math
import jax
import jax.numpy as jnp
from jax import lax
from jax.sharding import PartitionSpec as P

BLK = 128


def expand_rows(mask, row_ids, extent):
    labels = jnp.arange(mask.shape[0], dtype=jnp.int32)
    row_pick = ((row_ids // BLK)[:, None] == labels[None, :]).astype(jnp.float32)
    col_pick = ((jnp.arange(extent, dtype=jnp.int32) // BLK)[:, None] == labels[None, :]).astype(
        jnp.float32
    )
    return jnp.dot(jnp.dot(row_pick, mask.astype(jnp.float32)), col_pick.T)


def per_device(tokens, cotangent, w_first, w_second, mask_first, mask_second, gate_values):
    position = lax.axis_index("seq")
    extent = tokens.shape[1]
    channels = tokens.shape[2]
    shard_rows = w_first.shape[0]
    row_ids = position * shard_rows + jnp.arange(shard_rows, dtype=jnp.int32)
    keep_first = expand_rows(mask_first, row_ids, extent)
    keep_second = expand_rows(mask_second, row_ids, extent)
    local_first = (w_first.astype(jnp.float32) * keep_first).astype(jnp.bfloat16)
    local_second = (w_second.astype(jnp.float32) * keep_second).astype(jnp.bfloat16)
    full = lax.all_gather(jnp.stack([local_first, local_second]), "seq", axis=1, tiled=True)
    full_first, full_second = (full[0], full[1])
    shards = extent // shard_rows
    flat_cot = cotangent.reshape(extent, -1)
    back_flat = lax.dot_general(
        full_second, flat_cot, (((0,), (0,)), ((), ())), preferred_element_type=jnp.float32
    )
    back_col = back_flat.astype(jnp.bfloat16).reshape(cotangent.shape)
    back_rows = lax.all_to_all(back_col, "seq", split_axis=0, concat_axis=1, tiled=True)
    tokens_late, back_col = lax.optimization_barrier((tokens, back_col))
    gate_full = gate_values.astype(jnp.float32)[:, :, None]
    gated = tokens_late.astype(jnp.float32) * gate_full
    hidden = jnp.einsum("ijc,kj->ikc", tokens_late, full_first, preferred_element_type=jnp.float32)
    mixed = (hidden * gated).astype(jnp.bfloat16)
    mixed, back_rows = lax.optimization_barrier((mixed, back_rows))
    columns = lax.all_to_all(mixed, "seq", split_axis=1, concat_axis=0, tiled=True)
    flat_cols = columns.reshape(extent, -1)
    back_float = back_rows.astype(jnp.float32)
    back_hidden = (back_float * gated).astype(jnp.bfloat16)
    direct = gate_full * back_float * hidden
    through = jnp.einsum("ikc,kj->ijc", back_hidden, full_first, preferred_element_type=jnp.float32)
    grad_tokens = (direct + through).astype(jnp.bfloat16)
    summed_first = lax.psum_scatter(
        jnp.einsum("ikc,ijc->kj", back_hidden, tokens_late, preferred_element_type=jnp.float32),
        "seq",
        scatter_dimension=0,
        tiled=True,
    )
    part_second = lax.dot_general(
        flat_cot, flat_cols, (((1,), (1,)), ((), ())), preferred_element_type=jnp.float32
    )
    spread = lax.all_to_all(
        part_second.reshape(shards, shard_rows, extent),
        "seq",
        split_axis=0,
        concat_axis=0,
        tiled=True,
    )
    summed_second = jnp.sum(spread, axis=0)
    factor = 1.0 / math.sqrt(extent * channels)
    grad_first = keep_first * summed_first * factor
    grad_second = keep_second * summed_second * factor
    return (grad_tokens, grad_first, grad_second)


def solution(mesh):
    in_specs = (
        P(("groups", "seq"), None, None),
        P("groups", "seq", None),
        P("seq", None),
        P("seq", None),
        P(),
        P(),
        P(("groups", "seq"), None),
    )
    out_specs = (
        P(("groups", "seq"), None, None),
        P(("groups", "seq"), None),
        P(("groups", "seq"), None),
    )
    return jax.shard_map(
        per_device, mesh=mesh, in_specs=in_specs, out_specs=out_specs, check_vma=False
    )
```

profile of v0, /device:TPU:0, one launch (start us, length us, event | category | flops | bytes accessed | tf_op | source)
XLA Modules:
  0.0 964.3 jit_solution(4726643977585891241)
XLA Ops:
  7.2 0.0 all-gather.2.cloned.1.call-start
  7.2 1.1 fusion.14
  8.3 0.0 copy-start.2
  8.3 1.1 fusion.17
  9.4 0.0 copy-start.4
  9.4 0.8 fusion.23
  10.2 0.6 pad_maximum_fusion
  10.9 0.0 all-gather.2.cloned.1.call-update
  10.9 18.5 %copy.21 = bf16[64,8,32,512]{3,1,2,0:T(8,128)(2,1)} copy(bf16[64,8,32,512]{3,2,1,0:T(8,128)(2,1)} %bitcast.58) | data formatting | bytes 33554432
  29.3 0.0 copy-done.2
  29.3 0.0 copy-done.4
  29.3 22.4 %all-gather.2.cloned.1.call-done = bf16[2,512,512]{2,1,0:T(8,128)(2,1)} async-done(((bf16[2,32,512]{2,1,0:T(8,128)(2,1)}), bf16[2,512,512]{2,1,0:T(8,128)(2,1)}) %all-gather.2.cloned.1.call-update) | async-done | bytes 1048592 | tf_op jit(solution)/shard_map/all_gather | solution.py:29
  51.7 15.8 %convolution_convert_fusion = bf16[512,16384]{1,0:T(8,128)(2,1)} fusion(bf16[512,16384]{1,0:T(8,128)(2,1)} %bitcast.53, bf16[2,512,512]{2,1,0:T(8,128)(2,1)} %all-gather.2.cloned.1.call-done), kind=kOutput, calls=%fused_computation.9 | convolution fusion | flops 8598323200 | bytes 34078720 | tf_op jit(solution)/shard_map/dot_general | solution.py:33
  67.5 16.6 %copy.22 = bf16[64,8,32,512]{3,2,1,0:T(8,128)(2,1)} copy(bf16[64,8,32,512]{3,1,2,0:T(8,128)(2,1)} %bitcast.55) | data formatting | bytes 33554432
  84.0 0.0 copy-start.6
  84.0 0.0 copy-start.1
  84.0 5.5 all-to-all-start
  89.5 0.0 copy-done.6
  89.5 0.0 copy-done.1
  89.6 28.2 %fusion.4 = (bf16[32,512,512]{2,1,0:T(8,128)(2,1)}, f32[512,32,512]{2,0,1:T(8,128)}) fusion(bf16[32,512,512]{2,1,0:T(8,128)(2,1)} %param.7, f32[32,512]{1,0:T(8,128)S(1)} %convert_element_type.43, bf16[2,512,512]{2,1,0:T(8,128)(2,1)S(1)} %copy-done.1), kind=kOutput, calls=%fused_computation.7 | convolution fusion | flops 8623489024 | bytes 84475904 | tf_op jit(solution)/shard_map/ijc,kj->ikc/dot_general | solution.py:41
  117.7 268.3 %all-to-all-done = bf16[512,32,512]{2,1,0:T(8,128)(2,1)} async-done(((bf16[512,32,512]{2,1,0:T(8,128)(2,1)}), bf16[512,32,512]{2,1,0:T(8,128)(2,1)}, u32[]{:S(2)}, u32[]{:S(2)}) %all-to-all-start) | async-done | bytes 16777248 | tf_op jit(solution)/shard_map/all_to_all | solution.py:37
  386.0 0.0 copy-start
  386.0 15.1 %copy.15 = bf16[16,32,32,512]{3,2,0,1:T(8,128)(2,1)} copy(bf16[16,32,32,512]{3,2,1,0:T(8,128)(2,1)} %bitcast.6) | data formatting | bytes 33554432 | tf_op jit(solution)/shard_map/all_to_all | solution.py:37
  401.1 1.8 copy-done
  402.9 26.5 %copy.17 = bf16[32,512,512]{2,0,1:T(8,128)(2,1)} copy(bf16[32,512,512]{2,1,0:T(8,128)(2,1)S(1)} %copy-done) | data formatting | bytes 33554432 | tf_op jit(solution)/shard_map/optimization_barrier | solution.py:43
  429.4 70.2 %all-to-all-start.1 = ((bf16[32,512,512]{2,0,1:T(8,128)(2,1)}), bf16[32,512,512]{2,0,1:T(8,128)(2,1)}, u32[]{:S(2)}, u32[]{:S(2)}) async-start(bf16[32,512,512]{2,0,1:T(8,128)(2,1)} %copy.17), calls=%async_computation.2 | async-start | bytes 33554432 | tf_op jit(solution)/shard_map/all_to_all | solution.py:44
  499.7 0.3 reduce-scatter.2.cloned.1.call-start
  499.9 24.1 %fusion.11 = f32[512,512]{1,0:T(8,128)} fusion(bf16[32,512,512]{2,1,0:T(8,128)(2,1)} %param.7, bf16[32,512,512]{2,1,0:T(8,128)(2,1)} %bitcast.59, f32[32,512]{1,0:T(8,128)S(1)} %convert_element_type.43), kind=kOutput, calls=%fused_computation.12 | convolution fusion | flops 8631877632 | bytes 34668544 | tf_op jit(solution)/shard_map/ikc,ijc->kj/dot_general | solution.py:52
  524.0 0.0 reduce-scatter.2.cloned.1.call-update
  524.1 278.7 %all-to-all-done.1 = bf16[32,512,512]{2,0,1:T(8,128)(2,1)} async-done(((bf16[32,512,512]{2,0,1:T(8,128)(2,1)}), bf16[32,512,512]{2,0,1:T(8,128)(2,1)}, u32[]{:S(2)}, u32[]{:S(2)}) %all-to-all-start.1) | async-done | bytes 16777248 | tf_op jit(solution)/shard_map/all_to_all | solution.py:44
  802.8 15.8 %copy.18 = bf16[32,16,32,512]{3,2,0,1:T(8,128)(2,1)S(1)} copy(bf16[32,16,32,512]{3,0,2,1:T(8,128)(2,1)} %bitcast.12) | data formatting | bytes 33554432 | tf_op jit(solution)/shard_map/all_to_all | solution.py:44
  818.6 12.2 %copy.23 = bf16[64,8,32,512]{3,1,2,0:T(8,128)(2,1)} copy(bf16[64,8,32,512]{3,2,1,0:T(8,128)(2,1)S(1)} %bitcast.57) | data formatting | bytes 33554432
  830.8 18.0 %fusion.36 = f32[512,512]{0,1:T(8,128)} fusion(bf16[512,16384]{1,0:T(8,128)(2,1)} %bitcast.61, bf16[512,16384]{1,0:T(8,128)(2,1)} %bitcast.54), kind=kOutput, calls=%fused_computation.46 | convolution fusion | flops 8589934592 | bytes 34603008 | tf_op jit(solution)/shard_map/dot_general | solution.py:57
  848.9 70.2 %all-to-all-start.2 = ((f32[16,32,512]{2,1,0:T(8,128)}), f32[16,32,512]{2,1,0:T(8,128)S(1)}, u32[]{:S(2)}, u32[]{:S(2)}) async-start(f32[16,32,512]{2,1,0:T(8,128)} %bitcast.15), calls=%async_computation.3 | async-start | bytes 2097152 | tf_op jit(solution)/shard_map/all_to_all | solution.py:60
  919.1 0.0 copy-start.5
  919.1 0.0 copy-start.3
  919.1 36.2 %fusion.2 = bf16[32,512,512]{2,1,0:T(8,128)(2,1)} fusion(bf16[32,512,512]{2,1,0:T(8,128)(2,1)} %bitcast.60, f32[512,32,512]{2,0,1:T(8,128)} %get-tuple-element.10, f32[32,512]{1,0:T(8,128)S(1)} %convert_element_type.43, bf16[32,512,512]{2,1,0:T(8,128)(2,1)} %param.7, bf16[2,512,512]{2,1,0:T(8,128)(2,1)S(1)} %copy-done.1), kind=kOutput, calls=%fused_computation.4 | convolution fusion | flops 8673820672 | bytes 101318656 | tf_op jit(solution)/shard_map/ikc,kj->ijc/dot_general | solution.py:49
  955.3 0.0 reduce-scatter.2.cloned.1.call-done
  955.3 0.0 copy-done.5
  955.3 1.5 multiply_multiply_fusion.1
  956.8 0.0 all-to-all-done.2
  956.8 0.1 reduce_sum.9
  956.9 0.0 copy-done.3
  956.9 0.6 multiply_multiply_fusion
  (3 shorter events, 0.0 us)
Async XLA Ops:
  7.2 44.5 %all-gather.2.cloned.1.call-start = ((), (), s32[]{:S(2)}) async-start(), calls=%async_computation.4 | async-start | bytes 1114112 | tf_op jit(solution)/shard_map/all_gather | solution.py:29
  8.3 21.0 %copy-start.2 = (f32[32,512]{1,0:T(8,128)}, f32[32,512]{1,0:T(8,128)S(1)}, u32[]{:S(2)}) copy-start(f32[32,512]{1,0:T(8,128)S(1)} %fusion.14) | copy-start | bytes 196612
  9.4 19.9 %copy-start.4 = (f32[32,512]{1,0:T(8,128)}, f32[32,512]{1,0:T(8,128)S(1)}, u32[]{:S(2)}) copy-start(f32[32,512]{1,0:T(8,128)S(1)} %fusion.17) | copy-start | bytes 196612
  84.0 5.5 copy-start.6
  84.0 5.5 copy-start.1
  84.0 302.0 %all-to-all-start = ((bf16[512,32,512]{2,1,0:T(8,128)(2,1)}), bf16[512,32,512]{2,1,0:T(8,128)(2,1)}, u32[]{:S(2)}, u32[]{:S(2)}) async-start(bf16[512,32,512]{2,1,0:T(8,128)(2,1)} %bitcast.56), calls=%async_computation | async-start | bytes 33554432 | tf_op jit(solution)/shard_map/all_to_all | solution.py:37
  386.0 16.9 %copy-start = (bf16[32,512,512]{2,1,0:T(8,128)(2,1)S(1)}, bf16[32,512,512]{2,1,0:T(8,128)(2,1)}, u32[]{:S(2)}) copy-start(bf16[32,512,512]{2,1,0:T(8,128)(2,1)} %get-tuple-element.8) | copy-start | bytes 50331652
  429.4 373.4 %all-to-all-start.1 = ((bf16[32,512,512]{2,0,1:T(8,128)(2,1)}), bf16[32,512,512]{2,0,1:T(8,128)(2,1)}, u32[]{:S(2)}, u32[]{:S(2)}) async-start(bf16[32,512,512]{2,0,1:T(8,128)(2,1)} %copy.17), calls=%async_computation.2 | async-start | bytes 33554432 | tf_op jit(solution)/shard_map/all_to_all | solution.py:44
  499.7 455.6 %reduce-scatter.2.cloned.1.call-start = ((), (), s32[]{:S(2)}) async-start(), calls=%async_computation.5 | async-start | bytes 1114112 | tf_op jit(solution)/shard_map/reduce_scatter | solution.py:51
  848.9 107.9 %all-to-all-start.2 = ((f32[16,32,512]{2,1,0:T(8,128)}), f32[16,32,512]{2,1,0:T(8,128)S(1)}, u32[]{:S(2)}, u32[]{:S(2)}) async-start(f32[16,32,512]{2,1,0:T(8,128)} %bitcast.15), calls=%async_computation.3 | async-start | bytes 2097152 | tf_op jit(solution)/shard_map/all_to_all | solution.py:60
  919.1 36.2 %copy-start.5 = (f32[32,512]{1,0:T(8,128)S(1)}, f32[32,512]{1,0:T(8,128)}, u32[]{:S(2)}) copy-start(f32[32,512]{1,0:T(8,128)} %copy-done.4) | copy-start | bytes 196612
  919.1 37.7 %copy-start.3 = (f32[32,512]{1,0:T(8,128)S(1)}, f32[32,512]{1,0:T(8,128)}, u32[]{:S(2)}) copy-start(f32[32,512]{1,0:T(8,128)} %copy-done.2) | copy-start | bytes 196612
Sparse Core Ops, SparseCore 0:
  11.0 40.6 all-gather.1
  524.2 257.9 reduce-scatter.1
where the time goes:
time: 965 us; the launch traced here: 964 us
  waiting for transfers between devices  569 us (59%)
  starting transfers between devices  146 us (15%)
  matrix products  124 us (13%)
  local copies, waits for them, and re-layouts  106 us (11%)
  between operations  14.2 us (1%)
    all_to_all x1, waiting for transfers between devices, per_device(): lax.all_to_all(mixed, 'seq', split_axis=1, concat_axis=0, tiled=True)  279 us
    all_to_all x1, waiting for transfers between devices, per_device(): lax.all_to_all(back_col, 'seq', split_axis=0, concat_axis=1, tiled=True)  268 us
    all_to_all x1, starting transfers between devices, per_device(): lax.all_to_all(part_second.reshape(shards, shard_rows, extent), 'seq', sp...  70.2 us
    all_to_all x1, starting transfers between devices, per_device(): lax.all_to_all(mixed, 'seq', split_axis=1, concat_axis=0, tiled=True)  70.2 us
    unnamed x17, local copies, waits for them, and re-layouts  49 us
    dot_general x1, matrix products, per_device(): jnp.einsum('ikc,kj->ijc', back_hidden, full_first, preferred_element_type...  36.2 us
    dot_general x1, matrix products, per_device(): jnp.einsum('ijc,kj->ikc', tokens_late, full_first, preferred_element_type...  28.2 us
    optimization_barrier x1, local copies, waits for them, and re-layouts, per_device(): mixed, back_rows = lax.optimization_barrier((mixed, back_rows))  26.5 us
  transfers between devices with their start and end apart: 5, of which 3 were waited for; matrix products, arithmetic and copies ran while one was open for 16% of the time, Pallas kernels for 0%

commit v1 on v0

--- a/solution.py
+++ b/solution.py
@@ -41,7 +41,10 @@
     hidden = jnp.einsum("ijc,kj->ikc", tokens_late, full_first, preferred_element_type=jnp.float32)
     mixed = (hidden * gated).astype(jnp.bfloat16)
     mixed, back_rows = lax.optimization_barrier((mixed, back_rows))
-    columns = lax.all_to_all(mixed, "seq", split_axis=1, concat_axis=0, tiled=True)
+    columns = jnp.concatenate(
+        lax.all_to_all(jnp.stack(jnp.split(mixed, lax.axis_size("seq"), axis=1)), "seq", 0, 0),
+        axis=0,
+    )
     flat_cols = columns.reshape(extent, -1)
     back_float = back_rows.astype(jnp.float32)
     back_hidden = (back_float * gated).astype(jnp.bfloat16)

time: 965 us -> 947 us (0.981)
  local copies, waits for them, and re-layouts: 106 us -> 88.1 us
    optimization_barrier x1 -> x0, local copies, waits for them, and re-layouts: 26.5 us -> none  [per_device(): mixed, back_rows = lax.optimization_barrier((mixed, back_rows))]
    unnamed x17 -> x32, local copies, waits for them, and re-layouts: 49 us -> 72 us
    all_to_all x1 -> x0, local copies, waits for them, and re-layouts: 15.8 us -> none  [per_device(): lax.all_to_all(mixed, 'seq', split_axis=1, concat_axis=0, tiled=True)]
  transfers between devices with their start and end apart: 5 -> 5, of which waited for: 3 -> 3; matrix products, arithmetic and copies ran while one was open for 16% -> 15% of each run, Pallas kernels for 0% -> 0%
where the time goes in v1:
time: 947 us; the launch traced here: 946 us
  waiting for transfers between devices  570 us (60%)
  starting transfers between devices  146 us (15%)
  matrix products  124 us (13%)
  local copies, waits for them, and re-layouts  88.1 us (9%)
  between operations  14.2 us (1%)
    all_to_all x1, waiting for transfers between devices, per_device(): lax.all_to_all(jnp.stack(jnp.split(mixed, lax.axis_size('seq'), axis=1)),...  279 us
    all_to_all x1, waiting for transfers between devices, per_device(): lax.all_to_all(back_col, 'seq', split_axis=0, concat_axis=1, tiled=True)  268 us
    unnamed x32, local copies, waits for them, and re-layouts  72 us
    all_to_all x1, starting transfers between devices, per_device(): lax.all_to_all(part_second.reshape(shards, shard_rows, extent), 'seq', sp...  70.2 us
    all_to_all x1, starting transfers between devices, per_device(): lax.all_to_all(jnp.stack(jnp.split(mixed, lax.axis_size('seq'), axis=1)),...  70.2 us
    dot_general x1, matrix products, per_device(): jnp.einsum('ikc,kj->ijc', back_hidden, full_first, preferred_element_type...  36.2 us
    dot_general x1, matrix products, per_device(): jnp.einsum('ijc,kj->ikc', tokens_late, full_first, preferred_element_type...  28.2 us
    dot_general x1, matrix products, per_device(): jnp.einsum('ikc,ijc->kj', back_hidden, tokens_late, preferred_element_typ...  24.1 us
  transfers between devices with their start and end apart: 5, of which 3 were waited for; matrix products, arithmetic and copies ran while one was open for 15% of the time, Pallas kernels for 0%

profile of v1, /device:TPU:0, one launch (start us, length us, event | category | flops | bytes accessed | tf_op | source)
XLA Modules:
  0.0 945.8 jit_solution(4492926866911777404)
XLA Ops:
  7.2 0.0 all-gather.2.cloned.1.call-start
  7.2 1.0 fusion.14
  8.2 1.0 fusion.17
  9.2 0.8 fusion.23
  10.0 0.6 pad_maximum_fusion
  10.7 0.0 all-gather.2.cloned.1.call-update
  10.7 18.5 %copy.14 = bf16[64,8,32,512]{3,1,2,0:T(8,128)(2,1)} copy(bf16[64,8,32,512]{3,2,1,0:T(8,128)(2,1)} %bitcast.87) | data formatting | bytes 33554432
  29.2 0.0 copy-done.2
  29.2 0.0 copy-done.4
  29.2 22.4 %all-gather.2.cloned.1.call-done = bf16[2,512,512]{2,1,0:T(8,128)(2,1)} async-done(((bf16[2,32,512]{2,1,0:T(8,128)(2,1)}), bf16[2,512,512]{2,1,0:T(8,128)(2,1)}) %all-gather.2.cloned.1.call-update) | async-done | bytes 1048592 | tf_op jit(solution)/shard_map/all_gather | solution.py:29
  51.5 15.8 %convolution_convert_fusion = bf16[512,16384]{1,0:T(8,128)(2,1)} fusion(bf16[512,16384]{1,0:T(8,128)(2,1)} %bitcast.83, bf16[2,512,512]{2,1,0:T(8,128)(2,1)} %all-gather.2.cloned.1.call-done), kind=kOutput, calls=%fused_computation.9 | convolution fusion | flops 8598323200 | bytes 34078720 | tf_op jit(solution)/shard_map/dot_general | solution.py:33
  67.3 16.6 %copy.15 = bf16[64,8,32,512]{3,2,1,0:T(8,128)(2,1)} copy(bf16[64,8,32,512]{3,1,2,0:T(8,128)(2,1)} %bitcast.85) | data formatting | bytes 33554432
  83.9 5.5 all-to-all-start
  89.3 0.0 copy-done.6
  89.4 28.2 %fusion.4 = (bf16[32,512,512]{2,1,0:T(8,128)(2,1)}, f32[512,32,512]{2,0,1:T(8,128)}) fusion(bf16[32,512,512]{2,1,0:T(8,128)(2,1)} %param.7, f32[32,512]{1,0:T(8,128)S(1)} %convert_element_type.43, bf16[2,512,512]{2,1,0:T(8,128)(2,1)S(1)} %copy-done.1), kind=kOutput, calls=%fused_computation.7 | convolution fusion | flops 8623489024 | bytes 84475904 | tf_op jit(solution)/shard_map/ijc,kj->ikc/dot_general | solution.py:41
  117.6 268.3 %all-to-all-done = bf16[512,32,512]{2,1,0:T(8,128)(2,1)} async-done(((bf16[512,32,512]{2,1,0:T(8,128)(2,1)}), bf16[512,32,512]{2,1,0:T(8,128)(2,1)}, u32[]{:S(2)}, u32[]{:S(2)}) %all-to-all-start) | async-done | bytes 16777248 | tf_op jit(solution)/shard_map/all_to_all | solution.py:37
  385.9 15.1 %copy.10 = bf16[16,32,32,512]{3,2,0,1:T(8,128)(2,1)} copy(bf16[16,32,32,512]{3,2,1,0:T(8,128)(2,1)} %bitcast.6) | data formatting | bytes 33554432 | tf_op jit(solution)/shard_map/all_to_all | solution.py:37
  400.9 1.8 copy-done
  402.7 1.1 bitcast_dynamic-update-slice_fusion.15
  403.8 1.1 bitcast_dynamic-update-slice_fusion.14
  404.9 1.1 bitcast_dynamic-update-slice_fusion.13
  406.1 1.1 bitcast_dynamic-update-slice_fusion.12
  407.2 1.1 bitcast_dynamic-update-slice_fusion.11
  408.3 1.1 bitcast_dynamic-update-slice_fusion.10
  409.4 1.1 bitcast_dynamic-update-slice_fusion.9
  410.5 1.1 bitcast_dynamic-update-slice_fusion.8
  411.6 1.2 bitcast_dynamic-update-slice_fusion.7
  412.8 1.1 bitcast_dynamic-update-slice_fusion.6
  413.8 1.1 bitcast_dynamic-update-slice_fusion.5
  414.9 1.1 bitcast_dynamic-update-slice_fusion.4
  416.1 1.2 bitcast_dynamic-update-slice_fusion.3
  417.2 1.1 bitcast_dynamic-update-slice_fusion.2
  418.3 1.1 bitcast_dynamic-update-slice_fusion.1
  419.4 1.1 bitcast_dynamic-update-slice_fusion
  420.5 70.2 %all-to-all-start.1 = ((bf16[16,32,32,512]{3,2,1,0:T(8,128)(2,1)}), bf16[16,32,32,512]{3,2,1,0:T(8,128)(2,1)}, u32[]{:S(2)}, u32[]{:S(2)}) async-start(bf16[16,32,32,512]{3,2,1,0:T(8,128)(2,1)} %bitcast_dynamic-update-slice_fusion), calls=%async_computation.2 | async-start | bytes 33554432 | tf_op jit(solution)/shard_map/all_to_all | solution.py:45
  490.8 0.0 reduce-scatter.2.cloned.1.call-start
  490.8 24.1 %fusion.11 = f32[512,512]{1,0:T(8,128)} fusion(bf16[32,512,512]{2,1,0:T(8,128)(2,1)} %param.7, bf16[32,512,512]{2,1,0:T(8,128)(2,1)} %bitcast.88, f32[32,512]{1,0:T(8,128)S(1)} %convert_element_type.43), kind=kOutput, calls=%fused_computation.12 | convolution fusion | flops 8631877632 | bytes 34668544 | tf_op jit(solution)/shard_map/ikc,ijc->kj/dot_general | solution.py:55
  514.9 0.0 reduce-scatter.2.cloned.1.call-update
  514.9 279.0 %all-to-all-done.1 = bf16[16,32,32,512]{3,2,1,0:T(8,128)(2,1)} async-done(((bf16[16,32,32,512]{3,2,1,0:T(8,128)(2,1)}), bf16[16,32,32,512]{3,2,1,0:T(8,128)(2,1)}, u32[]{:S(2)}, u32[]{:S(2)}) %all-to-all-start.1) | async-done | bytes 16777248 | tf_op jit(solution)/shard_map/all_to_all | solution.py:45
  793.9 18.4 %copy.16 = bf16[64,8,32,512]{3,1,2,0:T(8,128)(2,1)} copy(bf16[64,8,32,512]{3,2,1,0:T(8,128)(2,1)} %bitcast.38) | data formatting | bytes 33554432
  812.3 18.0 %fusion.36 = f32[512,512]{0,1:T(8,128)} fusion(bf16[512,16384]{1,0:T(8,128)(2,1)} %bitcast.90, bf16[512,16384]{1,0:T(8,128)(2,1)} %bitcast.84), kind=kOutput, calls=%fused_computation.62 | convolution fusion | flops 8589934592 | bytes 34603008 | tf_op jit(solution)/shard_map/dot_general | solution.py:60
  830.3 70.2 %all-to-all-start.2 = ((f32[16,32,512]{2,1,0:T(8,128)}), f32[16,32,512]{2,1,0:T(8,128)S(1)}, u32[]{:S(2)}, u32[]{:S(2)}) async-start(f32[16,32,512]{2,1,0:T(8,128)} %bitcast.29), calls=%async_computation.3 | async-start | bytes 2097152 | tf_op jit(solution)/shard_map/all_to_all | solution.py:63
  900.6 0.0 copy-start.5
  900.6 36.2 %fusion.2 = bf16[32,512,512]{2,1,0:T(8,128)(2,1)} fusion(bf16[32,512,512]{2,1,0:T(8,128)(2,1)} %bitcast.89, f32[512,32,512]{2,0,1:T(8,128)} %get-tuple-element.10, f32[32,512]{1,0:T(8,128)S(1)} %convert_element_type.43, bf16[32,512,512]{2,1,0:T(8,128)(2,1)} %param.7, bf16[2,512,512]{2,1,0:T(8,128)(2,1)S(1)} %copy-done.1), kind=kOutput, calls=%fused_computation.4 | convolution fusion | flops 8673820672 | bytes 101318656 | tf_op jit(solution)/shard_map/ikc,kj->ijc/dot_general | solution.py:52
  936.8 1.5 multiply_multiply_fusion.1
  938.3 0.0 all-to-all-done.2
  938.3 0.1 reduce_sum.9
  938.4 0.6 multiply_multiply_fusion
  (13 shorter events, 0.0 us)
Async XLA Ops:
  7.2 44.4 %all-gather.2.cloned.1.call-start = ((), (), s32[]{:S(2)}) async-start(), calls=%async_computation.4 | async-start | bytes 1114112 | tf_op jit(solution)/shard_map/all_gather | solution.py:29
  8.2 20.9 %copy-start.2 = (f32[32,512]{1,0:T(8,128)}, f32[32,512]{1,0:T(8,128)S(1)}, u32[]{:S(2)}) copy-start(f32[32,512]{1,0:T(8,128)S(1)} %fusion.14) | copy-start | bytes 196612
  9.2 19.9 %copy-start.4 = (f32[32,512]{1,0:T(8,128)}, f32[32,512]{1,0:T(8,128)S(1)}, u32[]{:S(2)}) copy-start(f32[32,512]{1,0:T(8,128)S(1)} %fusion.17) | copy-start | bytes 196612
  83.9 5.5 copy-start.6
  83.9 5.5 copy-start.1
  83.9 302.0 %all-to-all-start = ((bf16[512,32,512]{2,1,0:T(8,128)(2,1)}), bf16[512,32,512]{2,1,0:T(8,128)(2,1)}, u32[]{:S(2)}, u32[]{:S(2)}) async-start(bf16[512,32,512]{2,1,0:T(8,128)(2,1)} %bitcast.86), calls=%async_computation | async-start | bytes 33554432 | tf_op jit(solution)/shard_map/all_to_all | solution.py:37
  385.9 16.9 %copy-start = (bf16[32,512,512]{2,1,0:T(8,128)(2,1)S(1)}, bf16[32,512,512]{2,1,0:T(8,128)(2,1)}, u32[]{:S(2)}) copy-start(bf16[32,512,512]{2,1,0:T(8,128)(2,1)} %get-tuple-element.8) | copy-start | bytes 50331652
  420.5 373.4 %all-to-all-start.1 = ((bf16[16,32,32,512]{3,2,1,0:T(8,128)(2,1)}), bf16[16,32,32,512]{3,2,1,0:T(8,128)(2,1)}, u32[]{:S(2)}, u32[]{:S(2)}) async-start(bf16[16,32,32,512]{3,2,1,0:T(8,128)(2,1)} %bitcast_dynamic-update-slice_fusion), calls=%async_computation.2 | async-start | bytes 33554432 | tf_op jit(solution)/shard_map/all_to_all | solution.py:45
  490.8 446.0 %reduce-scatter.2.cloned.1.call-start = ((), (), s32[]{:S(2)}) async-start(), calls=%async_computation.5 | async-start | bytes 1114112 | tf_op jit(solution)/shard_map/reduce_scatter | solution.py:54
  830.3 107.9 %all-to-all-start.2 = ((f32[16,32,512]{2,1,0:T(8,128)}), f32[16,32,512]{2,1,0:T(8,128)S(1)}, u32[]{:S(2)}, u32[]{:S(2)}) async-start(f32[16,32,512]{2,1,0:T(8,128)} %bitcast.29), calls=%async_computation.3 | async-start | bytes 2097152 | tf_op jit(solution)/shard_map/all_to_all | solution.py:63
  900.6 36.2 %copy-start.5 = (f32[32,512]{1,0:T(8,128)S(1)}, f32[32,512]{1,0:T(8,128)}, u32[]{:S(2)}) copy-start(f32[32,512]{1,0:T(8,128)} %copy-done.4) | copy-start | bytes 196612
  900.6 37.8 %copy-start.3 = (f32[32,512]{1,0:T(8,128)S(1)}, f32[32,512]{1,0:T(8,128)}, u32[]{:S(2)}) copy-start(f32[32,512]{1,0:T(8,128)} %copy-done.2) | copy-start | bytes 196612
Sparse Core Ops, SparseCore 0:
  10.8 40.6 all-gather.1
  515.0 258.1 reduce-scatter.1
